TPU v7x, 512 devices: a whole 4x4x16 slice. The times are simulated.
512 devices in a mesh: rows: 8 (over x_lo, y), cols: 64 (over z, x_hi, core).
Axes of the slice: x: 4 (x_hi: 2, x_lo: 2; x = x_hi * 2 + x_lo), y: 4, z: 16, core: 2. Of those that a mesh axis runs over, the one named last changes fastest.
Arguments:
- points: bfloat16 [32, 16384], P(None, ('rows', 'cols')), may hold values from 0 to 1
- samples: bfloat16 [32, 32768], P(None, 'cols'), may hold values from -0.5 to 1.5
- potential: float32 [32768], P('cols'), may hold values from -6 to 60
Outputs:
- point_potential: float32 [16384], P(('rows', 'cols'))
- sample_potential: float32 [32768], P('cols')
- barycenter: float32 [32, 16384], P(None, ('rows', 'cols'))
All inputs are finite; a program needn't handle non-finite values.
Results may differ from a plain program's by a relative error of at most 0.00055.
Values may be sent and summed in bfloat16 or wider, within the bound.
No kernel may reach another device: no remote copies, remote signals or barrier semaphores. Data moves between devices by JAX's collectives and lax.ppermute only.
A program may use at most 64 MiB of HBM per device.

v0:
```python
import math
import jax
import jax.numpy as jnp
from jax import lax
from jax.sharding import PartitionSpec as P

EPS = 0.25


def joined(part, axis, combine):
    gathered = jax.tree.map(lambda a: lax.all_gather(a, axis), part)

    def take(source):
        return jax.tree.map(lambda a: lax.dynamic_index_in_dim(a, source, 0, False), gathered)

    return lax.fori_loop(
        1, lax.axis_size(axis), lambda source, state: combine(state, take(source)), take(0)
    )


def combine_stats(first, second):
    top = jnp.maximum(first[0], second[0])
    total = first[1] * jnp.exp(first[0] - top) + second[1] * jnp.exp(second[0] - top)
    return (top, total)


def on_device(points, samples, potential):
    own_count = points.shape[1]
    whole = lax.all_gather(points, "cols", axis=1, tiled=True)
    block_count = whole.shape[1]
    col_count = lax.axis_size("cols")
    total_samples = samples.shape[1] * col_count
    total_points = block_count * lax.axis_size("rows")
    xf = whole.astype(jnp.float32)
    yf = samples.astype(jnp.float32)
    point_sq = jnp.sum(xf * xf, axis=0)
    sample_sq = jnp.sum(yf * yf, axis=0)
    cross = lax.dot_general(
        whole, samples, (((0,), (0,)), ((), ())), preferred_element_type=jnp.float32
    )
    cost = 0.5 * point_sq[:, None] + 0.5 * sample_sq[None, :] - cross
    score = (potential[None, :] - cost) / EPS
    row_top = lax.pmax(jnp.max(score, axis=1), "cols")
    row_sum = lax.psum(jnp.sum(jnp.exp(score - row_top[:, None]), axis=1), "cols")
    point_full = -EPS * (row_top + jnp.log(row_sum) - math.log(total_samples))
    col_score = (point_full[:, None] - cost) / EPS
    col_top = jnp.max(col_score, axis=0)
    col_sum = jnp.sum(jnp.exp(col_score - col_top[None, :]), axis=0)
    col_top, col_sum = joined((col_top, col_sum), "rows", combine_stats)
    sample_potential = -EPS * (col_top + jnp.log(col_sum) - math.log(total_points))
    new_score = (sample_potential[None, :] - cost) / EPS
    block_top = jnp.max(new_score, axis=1)
    weight = jnp.exp(new_score - block_top[:, None]).astype(jnp.bfloat16)
    denom = jnp.sum(weight.astype(jnp.float32), axis=1)
    numer = lax.dot_general(
        samples, weight, (((1,), (1,)), ((), ())), preferred_element_type=jnp.float32
    )
    position = lax.axis_index("cols") * own_count
    new_top = lax.pmax(block_top, "cols")
    scale = jnp.exp(block_top - new_top)
    numer_scaled = numer * scale[None, :]
    denom_scaled = denom * scale
    numer_all, denom_all = lax.psum((numer_scaled, denom_scaled), "cols")
    numer_own = lax.dynamic_slice_in_dim(numer_all, position, own_count, 1)
    denom_own = lax.dynamic_slice_in_dim(denom_all, position, own_count, 0)
    barycenter = numer_own / denom_own[None, :]
    point_potential = lax.dynamic_slice_in_dim(point_full, position, own_count, 0)
    return (point_potential, sample_potential, barycenter)


def solution(mesh):
    placed = (P(None, ("rows", "cols")), P(None, "cols"), P("cols"))
    return jax.shard_map(
        on_device,
        mesh=mesh,
        in_specs=placed,
        out_specs=(P(("rows", "cols")), P("cols"), P(None, ("rows", "cols"))),
        check_vma=False,
    )
```

profile of v0, /device:TPU:1, one launch (start us, length us, event | category | flops | bytes accessed | tf_op | source)
XLA Modules:
  0.0 1036.2 jit_solution(15728335356451031905)
XLA Ops:
  7.2 0.0 copy-start.4
  7.2 0.0 all-reduce.2.cloned.1.call-start
  7.2 0.8 multiply_reduce_fusion.1
  8.0 0.8 copy.6
  8.8 86.0 %all_gather.15 = bf16[32,2048]{0,1:T(8,128)(2,1)S(1)} all-gather(bf16[32,32]{0,1:T(8,128)(2,1)S(1)} %copy.6), channel_id=1, replica_groups=mesh['rows'=8,'cols'=64] {'cols'}, dimensions={1}, use_global_device_ids=true | all-gather | bytes 133120 | tf_op jit(solution)/shard_map/all_gather | solution.py:29
  94.8 0.3 multiply_reduce_fusion
  95.2 3.6 fusion
  98.8 130.3 %pmax.14 = f32[2048]{0:T(1024)S(1)} all-reduce(f32[2048]{0:T(1024)S(1)} %get-tuple-element.156), channel_id=1, replica_groups=mesh['rows'=8,'cols'=64] {'cols'}, use_global_device_ids=true, to_apply=%region_3.0 | all-reduce | flops 2048 | bytes 16384 | tf_op jit(solution)/shard_map/pmax | solution.py:43
  229.1 0.0 copy-done.4
  229.1 3.1 exponential_reduce_fusion.1
  232.2 131.1 %psum.21 = f32[2048]{0:T(1024)S(1)} all-reduce(f32[2048]{0:T(1024)S(1)} %exponential_reduce_fusion.1), channel_id=1, replica_groups=mesh['rows'=8,'cols'=64] {'cols'}, use_global_device_ids=true, to_apply=%region_5.0 | all-reduce | flops 2048 | bytes 16384 | tf_op jit(solution)/shard_map/psum | solution.py:44
  363.4 0.0 copy-start
  363.4 2.8 fusion.1
  366.2 0.6 copy-done
  366.8 0.9 exponential_reduce_fusion
  367.7 19.0 %all-gather.2 = f32[8,1,512]{2,1,0:T(1,128)S(1)} all-gather(f32[1,1,512]{2,1,0:T(1,128)S(1)} %bitcast.28), channel_id=2, replica_groups=mesh['rows'=8,'cols'=64] {'rows'}, dimensions={0}, use_global_device_ids=true | all-gather | bytes 18432 | tf_op jit(solution)/shard_map/all_gather | solution.py:11
  386.8 19.0 %all-gather.3 = f32[8,1,512]{2,1,0:T(1,128)S(1)} all-gather(f32[1,1,512]{2,1,0:T(1,128)S(1)} %bitcast.29), channel_id=3, replica_groups=mesh['rows'=8,'cols'=64] {'rows'}, dimensions={0}, use_global_device_ids=true | all-gather | bytes 18432 | tf_op jit(solution)/shard_map/all_gather | solution.py:11
  405.8 0.4 while.17
  406.2 0.0 copy-start.1
  406.2 0.0 copy-start.3
  406.3 2.8 fusion.2
  409.1 0.6 copy-done.1
  409.7 0.0 copy-start.2
  409.7 1.1 convert_reduce_fusion
  410.8 0.0 copy-done.3
  410.8 140.0 %pmax.15 = f32[2048]{0:T(1024)S(1)} all-reduce(f32[2048]{0:T(1024)S(1)} %fusion.2), channel_id=1, replica_groups=mesh['rows'=8,'cols'=64] {'cols'}, use_global_device_ids=true, to_apply=%region_11.12 | all-reduce | flops 2048 | bytes 16384 | tf_op jit(solution)/shard_map/pmax | solution.py:59
  550.8 0.0 copy-done.2
  550.8 1.2 fusion.3
  552.0 0.0 all-reduce.2.cloned.1.call-update
  552.0 0.6 dynamic_slice.36
  552.6 130.8 %psum.23 = f32[2048]{0:T(1024)S(1)} all-reduce(f32[2048]{0:T(1024)S(1)} %get-tuple-element.150), channel_id=1, replica_groups=mesh['rows'=8,'cols'=64] {'cols'}, use_global_device_ids=true, to_apply=%region_14.15 | all-reduce | flops 2048 | bytes 16384 | tf_op jit(solution)/shard_map/psum | solution.py:63
  683.4 0.1 dynamic_slice.40
  683.5 344.5 %all-reduce.2.cloned.1.call-done = f32[32,2048]{1,0:T(8,128)} async-done(((f32[32,2048]{1,0:T(8,128)}), f32[32,2048]{1,0:T(8,128)}) %all-reduce.2.cloned.1.call-update) | async-done | bytes 262160 | tf_op jit(solution)/shard_map/psum | solution.py:63
  1028.0 1.4 dynamic-slice_divide_fusion
  (23 shorter events, 0.3 us)
Async XLA Ops:
  7.2 221.9 %copy-start.4 = (f32[512]{0:T(512)S(1)}, f32[512]{0:T(512)}, u32[]{:S(2)}) copy-start(f32[512]{0:T(512)} %param.7) | copy-start | bytes 6148
  7.2 1020.8 %all-reduce.2.cloned.1.call-start = ((), (), s32[]{:S(2)}) async-start(), calls=%async_computation | async-start | bytes 524288 | tf_op jit(solution)/shard_map/psum | solution.py:63
  363.4 3.5 copy-start
  406.2 3.5 copy-start.1
  406.2 4.5 copy-start.3
  409.7 141.1 %copy-start.2 = (bf16[32,512]{1,0:T(8,128)(2,1)S(1)}, bf16[32,512]{1,0:T(8,128)(2,1)}, u32[]{:S(2)}) copy-start(bf16[32,512]{1,0:T(8,128)(2,1)} %param.6) | copy-start | bytes 98308
Sparse Core Ops, SparseCore 0:
  552.1 475.8 all-reduce.1
where the time goes:
time: 1040 us
  blocking collectives  656 us (63%)
  waiting for transfers between devices  345 us (33%)
  between operations  14.2 us (1%)
  other arithmetic  13.5 us (1%)
    psum x1, waiting for transfers between devices, on_device(): numer_all, denom_all = lax.psum((numer_scaled, denom_scaled), 'cols')  344 us
    pmax x1, blocking collectives, on_device(): new_top = lax.pmax(block_top, 'cols')  140 us
    psum x1, blocking collectives, on_device(): lax.psum(jnp.sum(jnp.exp(score - row_top[:, None]), axis=1), 'cols')  131 us
    psum x1, blocking collectives, on_device(): numer_all, denom_all = lax.psum((numer_scaled, denom_scaled), 'cols')  131 us
    pmax x1, blocking collectives, on_device(): row_top = lax.pmax(jnp.max(score, axis=1), 'cols')  130 us
    all_gather x1, blocking collectives, on_device(): whole = lax.all_gather(points, 'cols', axis=1, tiled=True)  86 us
    all_gather x2, blocking collectives, joined(): gathered = jax.tree.map(lambda a: lax.all_gather(a, axis), part)  38.1 us
  transfers between devices with their start and end apart: 1, of which 1 were waited for; matrix products, arithmetic and copies ran while one was open for 0% of the time, Pallas kernels for 0%

commit v1 on v0

--- a/solution.py
+++ b/solution.py
@@ -41,7 +41,9 @@
     cost = 0.5 * point_sq[:, None] + 0.5 * sample_sq[None, :] - cross
     score = (potential[None, :] - cost) / EPS
     row_top = lax.pmax(jnp.max(score, axis=1), "cols")
-    row_sum = lax.psum(jnp.sum(jnp.exp(score - row_top[:, None]), axis=1), "cols")
+    row_sum = jnp.sum(
+        lax.all_gather(jnp.sum(jnp.exp(score - row_top[:, None]), axis=1), "cols"), axis=0
+    )
     point_full = -EPS * (row_top + jnp.log(row_sum) - math.log(total_samples))
     col_score = (point_full[:, None] - cost) / EPS
     col_top = jnp.max(col_score, axis=0)

time: 1040 us -> 979 us (0.941)
  blocking collectives: 656 us -> 598 us
    psum x1 -> x0, blocking collectives: 131 us -> none  [on_device(): lax.psum(jnp.sum(jnp.exp(score - row_top[:, None]), axis=1), 'cols')]
    all_gather x0 -> x1, blocking collectives: none -> 73.6 us  [on_device(): lax.all_gather(jnp.sum(jnp.exp(score - row_top[:, None]), axis=1), 'cols')]
where the time goes in v1:
time: 979 us; the launch traced here: 978 us
  blocking collectives  598 us (61%)
  waiting for transfers between devices  345 us (35%)
  between operations  14.2 us (1%)
  other arithmetic  13.5 us (1%)
    psum x1, waiting for transfers between devices, on_device(): numer_all, denom_all = lax.psum((numer_scaled, denom_scaled), 'cols')  345 us
    pmax x1, blocking collectives, on_device(): new_top = lax.pmax(block_top, 'cols')  140 us
    psum x1, blocking collectives, on_device(): numer_all, denom_all = lax.psum((numer_scaled, denom_scaled), 'cols')  131 us
    pmax x1, blocking collectives, on_device(): row_top = lax.pmax(jnp.max(score, axis=1), 'cols')  130 us
    all_gather x1, blocking collectives, on_device(): whole = lax.all_gather(points, 'cols', axis=1, tiled=True)  86 us
    all_gather x1, blocking collectives, on_device(): lax.all_gather(jnp.sum(jnp.exp(score - row_top[:, None]), axis=1), 'cols')  73.6 us
    all_gather x2, blocking collectives, joined(): gathered = jax.tree.map(lambda a: lax.all_gather(a, axis), part)  38.1 us
  transfers between devices with their start and end apart: 1, of which 1 were waited for; matrix products, arithmetic and copies ran while one was open for 0% of the time, Pallas kernels for 0%

profile of v1, /device:TPU:1, one launch (start us, length us, event | category | flops | bytes accessed | tf_op | source)
XLA Modules:
  0.0 978.3 jit_solution(7390617975656938329)
XLA Ops:
  7.2 0.0 copy-start.4
  7.2 0.0 all-reduce.2.cloned.1.call-start
  7.2 0.8 multiply_reduce_fusion.1
  8.0 0.8 copy.7
  8.8 86.0 %all_gather.21 = bf16[32,2048]{0,1:T(8,128)(2,1)S(1)} all-gather(bf16[32,32]{0,1:T(8,128)(2,1)S(1)} %copy.7), channel_id=1, replica_groups=mesh['rows'=8,'cols'=64] {'cols'}, dimensions={1}, use_global_device_ids=true | all-gather | bytes 133120 | tf_op jit(solution)/shard_map/all_gather | solution.py:29
  94.8 0.3 multiply_reduce_fusion
  95.2 3.6 fusion
  98.8 130.3 %pmax.14 = f32[2048]{0:T(1024)S(1)} all-reduce(f32[2048]{0:T(1024)S(1)} %get-tuple-element.156), channel_id=1, replica_groups=mesh['rows'=8,'cols'=64] {'cols'}, use_global_device_ids=true, to_apply=%region_3.0 | all-reduce | flops 2048 | bytes 16384 | tf_op jit(solution)/shard_map/pmax | solution.py:43
  229.1 0.0 copy-done.4
  229.1 3.1 exponential_reduce_fusion.1
  232.2 73.6 %all-gather = f32[131072]{0:T(1024)S(1)} all-gather(f32[2048]{0:T(1024)S(1)} %exponential_reduce_fusion.1), channel_id=2, replica_groups=mesh['rows'=8,'cols'=64] {'cols'}, dimensions={0}, use_global_device_ids=true | all-gather | bytes 532480 | tf_op jit(solution)/shard_map/all_gather | solution.py:45
  305.8 0.1 reshape.22
  305.9 0.0 copy-start
  306.0 2.8 fusion.1
  308.8 0.6 copy-done
  309.4 0.9 exponential_reduce_fusion
  310.3 19.0 %all-gather.3 = f32[8,1,512]{2,1,0:T(1,128)S(1)} all-gather(f32[1,1,512]{2,1,0:T(1,128)S(1)} %bitcast.28), channel_id=3, replica_groups=mesh['rows'=8,'cols'=64] {'rows'}, dimensions={0}, use_global_device_ids=true | all-gather | bytes 18432 | tf_op jit(solution)/shard_map/all_gather | solution.py:11
  329.4 19.0 %all-gather.4 = f32[8,1,512]{2,1,0:T(1,128)S(1)} all-gather(f32[1,1,512]{2,1,0:T(1,128)S(1)} %bitcast.29), channel_id=4, replica_groups=mesh['rows'=8,'cols'=64] {'rows'}, dimensions={0}, use_global_device_ids=true | all-gather | bytes 18432 | tf_op jit(solution)/shard_map/all_gather | solution.py:11
  348.4 0.4 while.17
  348.8 0.0 copy-start.1
  348.8 0.0 copy-start.3
  348.8 2.8 fusion.2
  351.7 0.6 copy-done.1
  352.2 0.0 copy-start.2
  352.2 1.1 convert_reduce_fusion
  353.3 0.0 copy-done.3
  353.3 139.6 %pmax.15 = f32[2048]{0:T(1024)S(1)} all-reduce(f32[2048]{0:T(1024)S(1)} %fusion.2), channel_id=1, replica_groups=mesh['rows'=8,'cols'=64] {'cols'}, use_global_device_ids=true, to_apply=%region_11.12 | all-reduce | flops 2048 | bytes 16384 | tf_op jit(solution)/shard_map/pmax | solution.py:61
  492.9 0.0 copy-done.2
  492.9 1.2 fusion.3
  494.1 0.0 all-reduce.2.cloned.1.call-update
  494.1 0.6 dynamic_slice.36
  494.7 130.7 %psum.15 = f32[2048]{0:T(1024)S(1)} all-reduce(f32[2048]{0:T(1024)S(1)} %get-tuple-element.150), channel_id=1, replica_groups=mesh['rows'=8,'cols'=64] {'cols'}, use_global_device_ids=true, to_apply=%region_14.15 | all-reduce | flops 2048 | bytes 16384 | tf_op jit(solution)/shard_map/psum | solution.py:65
  625.4 0.1 dynamic_slice.40
  625.5 344.5 %all-reduce.2.cloned.1.call-done = f32[32,2048]{1,0:T(8,128)} async-done(((f32[32,2048]{1,0:T(8,128)}), f32[32,2048]{1,0:T(8,128)}) %all-reduce.2.cloned.1.call-update) | async-done | bytes 262160 | tf_op jit(solution)/shard_map/psum | solution.py:65
  970.0 1.4 dynamic-slice_divide_fusion
  (24 shorter events, 0.3 us)
Async XLA Ops:
  7.2 221.9 %copy-start.4 = (f32[512]{0:T(512)S(1)}, f32[512]{0:T(512)}, u32[]{:S(2)}) copy-start(f32[512]{0:T(512)} %param.7) | copy-start | bytes 6148
  7.2 962.8 %all-reduce.2.cloned.1.call-start = ((), (), s32[]{:S(2)}) async-start(), calls=%async_computation | async-start | bytes 524288 | tf_op jit(solution)/shard_map/psum | solution.py:65
  305.9 3.5 copy-start
  348.8 3.5 copy-start.1
  348.8 4.5 copy-start.3
  352.2 140.7 %copy-start.2 = (bf16[32,512]{1,0:T(8,128)(2,1)S(1)}, bf16[32,512]{1,0:T(8,128)(2,1)}, u32[]{:S(2)}) copy-start(bf16[32,512]{1,0:T(8,128)(2,1)} %param.6) | copy-start | bytes 98308
Sparse Core Ops, SparseCore 0:
  494.2 475.7 all-reduce.1

commit v2 on v0

--- a/solution.py
+++ b/solution.py
@@ -26,7 +26,9 @@
 
 def on_device(points, samples, potential):
     own_count = points.shape[1]
-    whole = lax.all_gather(points, "cols", axis=1, tiled=True)
+    whole = jnp.concatenate(
+        lax.all_to_all(jnp.stack([points] * lax.axis_size("cols")), "cols", 0, 0), axis=1
+    )
     block_count = whole.shape[1]
     col_count = lax.axis_size("cols")
     total_samples = samples.shape[1] * col_count

time: 1040 us -> 987 us (0.949)
  blocking collectives: 656 us -> 571 us
  starting transfers between devices: 0.04 us -> 19.7 us
  waiting for transfers between devices: 345 us -> 360 us
    all_gather x1 -> x0, blocking collectives: 86 us -> none  [on_device(): whole = lax.all_gather(points, 'cols', axis=1, tiled=True)]
    all_to_all x0 -> x1, starting transfers between devices: none -> 19.6 us  [on_device(): lax.all_to_all(jnp.stack([points] * lax.axis_size('cols')), 'cols', 0, 0)]
    all_to_all x0 -> x1, waiting for transfers between devices: none -> 17.8 us  [on_device(): lax.all_to_all(jnp.stack([points] * lax.axis_size('cols')), 'cols', 0, 0)]
  transfers between devices with their start and end apart: 1 -> 2, of which waited for: 1 -> 2; matrix products, arithmetic and copies ran while one was open for 0% -> 0% of each run, Pallas kernels for 0% -> 0%
where the time goes in v2:
time: 987 us
  blocking collectives  571 us (58%)
  waiting for transfers between devices  360 us (36%)
  starting transfers between devices  19.7 us (2%)
  between operations  14.2 us (1%)
  other arithmetic  13.3 us (1%)
    psum x1, waiting for transfers between devices, on_device(): numer_all, denom_all = lax.psum((numer_scaled, denom_scaled), 'cols')  342 us
    pmax x1, blocking collectives, on_device(): new_top = lax.pmax(block_top, 'cols')  140 us
    psum x1, blocking collectives, on_device(): lax.psum(jnp.sum(jnp.exp(score - row_top[:, None]), axis=1), 'cols')  131 us
    psum x1, blocking collectives, on_device(): numer_all, denom_all = lax.psum((numer_scaled, denom_scaled), 'cols')  131 us
    pmax x1, blocking collectives, on_device(): row_top = lax.pmax(jnp.max(score, axis=1), 'cols')  130 us
    all_gather x2, blocking collectives, joined(): gathered = jax.tree.map(lambda a: lax.all_gather(a, axis), part)  38.1 us
  transfers between devices with their start and end apart: 2, of which 2 were waited for; matrix products, arithmetic and copies ran while one was open for 0% of the time, Pallas kernels for 0%

profile of v2, /device:TPU:1, one launch (start us, length us, event | category | flops | bytes accessed | tf_op | source)
XLA Modules:
  0.0 986.8 jit_solution(2812798826475804950)
XLA Ops:
  7.2 0.0 copy-start.2
  7.2 0.0 copy-start.4
  7.2 0.8 stack.2
  8.0 1.1 reshape.52
  9.0 19.6 %all-to-all-start = ((bf16[64,2,512]{2,1,0:T(2,128)(2,1)}), bf16[64,2,512]{2,1,0:T(2,128)(2,1)S(1)}, u32[]{:S(2)}, u32[]{:S(2)}) async-start(bf16[64,2,512]{2,1,0:T(2,128)(2,1)} %reshape.52), calls=%async_computation | async-start | bytes 262144 | tf_op jit(solution)/shard_map/all_to_all | solution.py:30
  28.6 0.0 all-reduce.2.cloned.1.call-start
  28.7 0.8 multiply_reduce_fusion.1
  29.5 17.8 %all-to-all-done = bf16[64,2,512]{2,1,0:T(2,128)(2,1)S(1)} async-done(((bf16[64,2,512]{2,1,0:T(2,128)(2,1)}), bf16[64,2,512]{2,1,0:T(2,128)(2,1)S(1)}, u32[]{:S(2)}, u32[]{:S(2)}) %all-to-all-start) | async-done | bytes 131104 | tf_op jit(solution)/shard_map/all_to_all | solution.py:30
  47.2 0.3 reshape.53
  47.5 0.2 multiply_reduce_fusion
  47.8 0.1 mul.84
  47.8 0.2 copy.6
  48.0 0.5 reshape.37
  48.6 0.0 copy-done.2
  48.6 0.0 copy-done.4
  48.6 2.9 fusion
  51.5 130.5 %pmax.14 = f32[2048]{0:T(1024)S(1)} all-reduce(f32[2048]{0:T(1024)S(1)} %get-tuple-element.156), channel_id=1, replica_groups=mesh['rows'=8,'cols'=64] {'cols'}, use_global_device_ids=true, to_apply=%region_3.0 | all-reduce | flops 2048 | bytes 16384 | tf_op jit(solution)/shard_map/pmax | solution.py:45
  182.0 3.1 exponential_reduce_fusion.1
  185.1 131.3 %psum.21 = f32[2048]{0:T(1024)S(1)} all-reduce(f32[2048]{0:T(1024)S(1)} %exponential_reduce_fusion.1), channel_id=1, replica_groups=mesh['rows'=8,'cols'=64] {'cols'}, use_global_device_ids=true, to_apply=%region_5.0 | all-reduce | flops 2048 | bytes 16384 | tf_op jit(solution)/shard_map/psum | solution.py:46
  316.4 0.0 copy-start
  316.4 2.8 fusion.1
  319.2 0.6 copy-done
  319.8 0.9 exponential_reduce_fusion
  320.8 19.0 %all-gather.2 = f32[8,1,512]{2,1,0:T(1,128)S(1)} all-gather(f32[1,1,512]{2,1,0:T(1,128)S(1)} %bitcast.31), channel_id=2, replica_groups=mesh['rows'=8,'cols'=64] {'rows'}, dimensions={0}, use_global_device_ids=true | all-gather | bytes 18432 | tf_op jit(solution)/shard_map/all_gather | solution.py:11
  339.8 19.0 %all-gather.3 = f32[8,1,512]{2,1,0:T(1,128)S(1)} all-gather(f32[1,1,512]{2,1,0:T(1,128)S(1)} %bitcast.32), channel_id=3, replica_groups=mesh['rows'=8,'cols'=64] {'rows'}, dimensions={0}, use_global_device_ids=true | all-gather | bytes 18432 | tf_op jit(solution)/shard_map/all_gather | solution.py:11
  358.9 0.4 while.17
  359.3 0.0 copy-start.1
  359.3 0.0 copy-start.3
  359.3 2.8 fusion.2
  362.1 0.6 copy-done.1
  362.7 1.0 convert_reduce_fusion
  363.8 0.0 copy-done.3
  363.8 140.0 %pmax.15 = f32[2048]{0:T(1024)S(1)} all-reduce(f32[2048]{0:T(1024)S(1)} %fusion.2), channel_id=1, replica_groups=mesh['rows'=8,'cols'=64] {'cols'}, use_global_device_ids=true, to_apply=%region_11.12 | all-reduce | flops 2048 | bytes 16384 | tf_op jit(solution)/shard_map/pmax | solution.py:61
  503.8 1.2 fusion.3
  505.0 0.0 all-reduce.2.cloned.1.call-update
  505.0 0.6 dynamic_slice.36
  505.6 130.8 %psum.23 = f32[2048]{0:T(1024)S(1)} all-reduce(f32[2048]{0:T(1024)S(1)} %get-tuple-element.150), channel_id=1, replica_groups=mesh['rows'=8,'cols'=64] {'cols'}, use_global_device_ids=true, to_apply=%region_14.15 | all-reduce | flops 2048 | bytes 16384 | tf_op jit(solution)/shard_map/psum | solution.py:65
  636.4 0.1 dynamic_slice.40
  636.4 342.1 %all-reduce.2.cloned.1.call-done = f32[32,2048]{1,0:T(8,128)} async-done(((f32[32,2048]{1,0:T(8,128)}), f32[32,2048]{1,0:T(8,128)}) %all-reduce.2.cloned.1.call-update) | async-done | bytes 262160 | tf_op jit(solution)/shard_map/psum | solution.py:65
  978.6 1.4 dynamic-slice_divide_fusion
  (23 shorter events, 0.3 us)
Async XLA Ops:
  7.2 41.4 %copy-start.2 = (bf16[32,512]{1,0:T(8,128)(2,1)S(1)}, bf16[32,512]{1,0:T(8,128)(2,1)}, u32[]{:S(2)}) copy-start(bf16[32,512]{1,0:T(8,128)(2,1)} %param.6) | copy-start | bytes 98308
  7.2 41.4 %copy-start.4 = (f32[512]{0:T(512)S(1)}, f32[512]{0:T(512)}, u32[]{:S(2)}) copy-start(f32[512]{0:T(512)} %param.7) | copy-start | bytes 6148
  9.0 38.2 %all-to-all-start = ((bf16[64,2,512]{2,1,0:T(2,128)(2,1)}), bf16[64,2,512]{2,1,0:T(2,128)(2,1)S(1)}, u32[]{:S(2)}, u32[]{:S(2)}) async-start(bf16[64,2,512]{2,1,0:T(2,128)(2,1)} %reshape.52), calls=%async_computation | async-start | bytes 262144 | tf_op jit(solution)/shard_map/all_to_all | solution.py:30
  28.6 949.9 %all-reduce.2.cloned.1.call-start = ((), (), s32[]{:S(2)}) async-start(), calls=%async_computation.1 | async-start | bytes 524288 | tf_op jit(solution)/shard_map/psum | solution.py:65
  316.4 3.5 copy-start
  359.3 3.5 copy-start.1
  359.3 4.5 copy-start.3
Sparse Core Ops, SparseCore 0:
  505.1 473.4 all-reduce.1
